TPU v7x, 32 devices: a whole 2x2x4 slice. The times are simulated.
32 devices in a mesh: rep: 8 (over z, x), rows: 4 (over y, core).
Axes of the slice: x: 2, y: 2, z: 4, core: 2. Of those that a mesh axis runs over, the one named last changes fastest.
Arguments:
- pooled_grad: bfloat16 [32768, 2, 128], P(('rep', 'rows')), may hold values from -6 to 6
- slot_source: int32 [32, 4, 1024], P(('rep', 'rows')), may hold values from 0 to 2047, as said below
- slot_target: int32 [32, 4, 1024], P(('rep', 'rows')), may hold values from 0 to 8191, as said below
- slot_count: int32 [32, 4], P(('rep', 'rows')), may hold values from 128 to 1024, as said below
- table_rows: float32 [2, 16384, 128], P(None, 'rows'), may hold values from -1.5 to 1.5
- accum: float32 [2, 16384], P(None, 'rows'), may hold values from 0.01 to 1
Outputs:
- new_rows: float32 [2, 16384, 128], P(None, 'rows')
- new_accum: float32 [2, 16384], P(None, 'rows')
Inputs may be any that keep to these rules, and one draw needn't show every extreme that they name: `slot_source`: entry q encodes a local sample q // 2 and a table q % 2; the table agrees with that of slot_target at the same slot. `slot_target`: entry t encodes a table t // 4096 and a row t % 4096 of the owner's shard; rows repeat across slots and senders. `slot_count`: slots at or past the count carry no lookup; every sender fills all slots to some owner.
All inputs are finite; a program needn't handle non-finite values.
Results may differ from a plain program's by a relative error of at most 0.0003.
Values may be sent and summed in bfloat16 or wider, within the bound.
A program may use at most 64 MiB of HBM per device.

v0:
```python
import math
import jax
import jax.numpy as jnp
from jax import lax
from jax.sharding import PartitionSpec as P

LEARN_RATE = 0.1
EPSILON = 1e-06


def accumulate(grads, targets, tables, rows_dev):
    feature = grads.shape[-1]
    flat_rows = grads.reshape(-1, feature)
    lookup_keys = targets.reshape(-1)
    row_total = tables * rows_dev
    block_size = math.gcd(row_total, 512)
    block_count = row_total // block_size
    offsets = jnp.arange(block_size, dtype=jnp.int32)

    def row_block(block_index):
        row_base = block_index * block_size
        matches = (lookup_keys[:, None] == row_base + offsets[None, :]).astype(jnp.bfloat16)
        return jnp.einsum("sr,sw->rw", matches, flat_rows, preferred_element_type=jnp.float32)

    blocks = lax.map(row_block, jnp.arange(block_count, dtype=jnp.int32))
    return blocks.reshape(tables, rows_dev, feature)


def pick_rows(flat_grad, lookup_keys):
    slot_total = lookup_keys.shape[0]
    block_size = math.gcd(slot_total, 1024)
    block_count = slot_total // block_size
    sources = jnp.arange(flat_grad.shape[0], dtype=jnp.int32)
    key_blocks = lookup_keys.reshape(block_count, block_size)

    def slot_block(block_keys):
        matches = (block_keys[:, None] == sources[None, :]).astype(jnp.bfloat16)
        return jnp.dot(matches, flat_grad, preferred_element_type=jnp.float32).astype(jnp.bfloat16)

    blocks = lax.map(slot_block, key_blocks)
    return blocks.reshape(slot_total, flat_grad.shape[1])


def adagrad(rows_part, state_part, row_grad):
    updated = state_part + jnp.mean(row_grad * row_grad, axis=2)
    shifted = rows_part - LEARN_RATE * row_grad / (jnp.sqrt(updated)[:, :, None] + EPSILON)
    return (shifted, updated)


def shards(pooled_grad, slot_source, slot_target, slot_count, table_rows, accum):
    tables = pooled_grad.shape[1]
    feature = pooled_grad.shape[2]
    rows_dev = table_rows.shape[1]
    owner_total = slot_source.shape[1]
    slot_total = slot_source.shape[2]
    flat_grad = pooled_grad.reshape(-1, feature)
    source = slot_source[0]
    target = slot_target[0]
    counts = slot_count[0]
    slot_ids = jnp.arange(slot_total, dtype=jnp.int32)
    filled = slot_ids[None, :] < counts[:, None]
    source_keys = jnp.where(filled, source, -1).reshape(-1)
    picked = pick_rows(flat_grad, source_keys).reshape(owner_total, slot_total, feature)
    targets = jnp.where(filled, target, -1)
    got_grads, got_targets = (
        lax.all_to_all(picked, "rows", split_axis=0, concat_axis=0, tiled=True),
        lax.all_to_all(targets, "rows", split_axis=0, concat_axis=0, tiled=True),
    )
    partial_grad = accumulate(got_grads, got_targets, tables, rows_dev)
    row_grad = lax.psum(partial_grad, "rep")
    new_rows, new_accum = adagrad(table_rows, accum, row_grad)
    return (new_rows, new_accum)


def solution(mesh):
    in_specs = (
        P(("rep", "rows"), None, None),
        P(("rep", "rows"), None, None),
        P(("rep", "rows"), None, None),
        P(("rep", "rows"), None),
        P(None, "rows", None),
        P(None, "rows"),
    )
    out_specs = (P(None, "rows", None), P(None, "rows"))
    return jax.shard_map(shards, mesh=mesh, in_specs=in_specs, out_specs=out_specs, check_vma=False)
```

profile of v0, /device:TPU:0, one launch (start us, length us, event | category | flops | bytes accessed | tf_op | source)
XLA Modules:
  0.0 295.6 jit_solution(14990334803559282214)
XLA Ops:
  7.2 1.4 compare_select_fusion
  8.6 4.3 %all-to-all-start = ((s32[4,1,1024]{2,1,0:T(1,128)}), s32[4,1,1024]{2,1,0:T(1,128)S(1)}, u32[]{:S(2)}, u32[]{:S(2)}) async-start(s32[4,1,1024]{2,1,0:T(1,128)} %compare_select_fusion), calls=%async_computation | async-start | bytes 32768 | tf_op jit(solution)/shard_map/all_to_all | solution.py:67
  12.8 0.8 bitcast_select_fusion
  13.6 12.9 %while.22 = (s32[]{:T(128)}, bf16[4,1024,128]{2,1,0:T(8,128)(2,1)}, s32[4,1024]{1,0:T(4,128)S(1)}, bf16[2048,128]{1,0:T(8,128)(2,1)}, s32[]{:T(128)}) while((s32[]{:T(128)}, bf16[4,1024,128]{2,1,0:T(8,128)(2,1)}, s32[4,1024]{1,0:T(4,128)S(1)}, bf16[2048,128]{1,0:T(8,128)(2,1)}, s32[]{:T(128)}) %tuple.52), condition=%wide.region_1.2_spmd.clone, body=%wide.region_0.1_spmd.clone.sunk | while | flops 539099136 | bytes 799297 | solution.py:40
  13.6 3.2 %fusion.27 = bf16[4,1024,128]{2,1,0:T(8,128)(2,1)} fusion(bf16[4,1024,128]{2,1,0:T(8,128)(2,1)} %get-tuple-element.167, s32[]{:T(128)} %get-tuple-element.166, bf16[2048,128]{1,0:T(8,128)(2,1)} %get-tuple-element.174, s32[1024]{0:T(1024)S(1)} %bitcast.46), kind=kOutput, calls=%fused_computation.7.clone.1 | convolution fusion | flops 539099136 | bytes 791040 | tf_op jit(solution)/shard_map/while/body/eval_jaxpr/dot_general | solution.py:38
  16.9 3.2 %fusion.27 = bf16[4,1024,128]{2,1,0:T(8,128)(2,1)} fusion(bf16[4,1024,128]{2,1,0:T(8,128)(2,1)} %get-tuple-element.167, s32[]{:T(128)} %get-tuple-element.166, bf16[2048,128]{1,0:T(8,128)(2,1)} %get-tuple-element.174, s32[1024]{0:T(1024)S(1)} %bitcast.46), kind=kOutput, calls=%fused_computation.7.clone.1 | convolution fusion | flops 539099136 | bytes 791040 | tf_op jit(solution)/shard_map/while/body/eval_jaxpr/dot_general | solution.py:38
  20.1 3.2 %fusion.27 = bf16[4,1024,128]{2,1,0:T(8,128)(2,1)} fusion(bf16[4,1024,128]{2,1,0:T(8,128)(2,1)} %get-tuple-element.167, s32[]{:T(128)} %get-tuple-element.166, bf16[2048,128]{1,0:T(8,128)(2,1)} %get-tuple-element.174, s32[1024]{0:T(1024)S(1)} %bitcast.46), kind=kOutput, calls=%fused_computation.7.clone.1 | convolution fusion | flops 539099136 | bytes 791040 | tf_op jit(solution)/shard_map/while/body/eval_jaxpr/dot_general | solution.py:38
  23.3 3.2 %fusion.27 = bf16[4,1024,128]{2,1,0:T(8,128)(2,1)} fusion(bf16[4,1024,128]{2,1,0:T(8,128)(2,1)} %get-tuple-element.167, s32[]{:T(128)} %get-tuple-element.166, bf16[2048,128]{1,0:T(8,128)(2,1)} %get-tuple-element.174, s32[1024]{0:T(1024)S(1)} %bitcast.46), kind=kOutput, calls=%fused_computation.7.clone.1 | convolution fusion | flops 539099136 | bytes 791040 | tf_op jit(solution)/shard_map/while/body/eval_jaxpr/dot_general | solution.py:38
  26.6 0.0 all-to-all-done
  26.6 3.5 %all-to-all-start.1 = ((bf16[4,1024,128]{2,1,0:T(8,128)(2,1)}), bf16[4,1024,128]{2,1,0:T(8,128)(2,1)S(1)}, u32[]{:S(2)}, u32[]{:S(2)}) async-start(bf16[4,1024,128]{2,1,0:T(8,128)(2,1)} %get-tuple-element.61), calls=%async_computation.1 | async-start | bytes 2097152 | tf_op jit(solution)/shard_map/all_to_all | solution.py:66
  30.1 0.0 all-reduce.2.cloned.1.call-start
  30.2 14.3 %all-to-all-done.1 = bf16[4,1024,128]{2,1,0:T(8,128)(2,1)S(1)} async-done(((bf16[4,1024,128]{2,1,0:T(8,128)(2,1)}), bf16[4,1024,128]{2,1,0:T(8,128)(2,1)S(1)}, u32[]{:S(2)}, u32[]{:S(2)}) %all-to-all-start.1) | async-done | bytes 1048608 | tf_op jit(solution)/shard_map/all_to_all | solution.py:66
  44.5 78.5 %while.23 = (s32[]{:T(128)}, f32[16,512,128]{2,1,0:T(8,128)}, s32[4,1024]{1,0:T(4,128)S(1)}, s32[16]{0:T(128)S(1)}, bf16[4096,128]{1,0:T(8,128)(2,1)S(1)}, /*index=5*/s32[]{:T(128)}, s32[1]{0:T(128)}) while((s32[]{:T(128)}, f32[16,512,128]{2,1,0:T(8,128)}, s32[4,1024]{1,0:T(4,128)S(1)}, s32[16]{0:T(128)S(1)}, ...), condition=%wide.region_3.4_spmd.clone, body=%wide.region_2.3_spmd.clone.sunk | while | flops 538968576 | bytes 1364585 | solution.py:25
  44.5 0.6 dynamic_slice.14
  45.7 3.7 %fusion.30 = f32[16,512,128]{2,1,0:T(8,128)} fusion(f32[16,512,128]{2,1,0:T(8,128)} %get-tuple-element.184, s32[]{:T(128)} %get-tuple-element.183, bf16[4096,128]{1,0:T(8,128)(2,1)S(1)} %get-tuple-element.194, s32[512]{0:T(512)S(1)} %iota_add_fusion.2, s32[4096]{0:T(1024)S(1)} %bitcast.45), kind=kOutput, calls=%fused_computation.14.clone.1 | convolution fusion | flops 538968064 | bytes 1329664 | tf_op jit(solution)/shard_map/while/body/eval_jaxpr/sr,sw->rw/dot_general | solution.py:23
  49.4 0.6 dynamic_slice.14
  50.7 3.7 %fusion.30 = f32[16,512,128]{2,1,0:T(8,128)} fusion(f32[16,512,128]{2,1,0:T(8,128)} %get-tuple-element.184, s32[]{:T(128)} %get-tuple-element.183, bf16[4096,128]{1,0:T(8,128)(2,1)S(1)} %get-tuple-element.194, s32[512]{0:T(512)S(1)} %iota_add_fusion.2, s32[4096]{0:T(1024)S(1)} %bitcast.45), kind=kOutput, calls=%fused_computation.14.clone.1 | convolution fusion | flops 538968064 | bytes 1329664 | tf_op jit(solution)/shard_map/while/body/eval_jaxpr/sr,sw->rw/dot_general | solution.py:23
  54.3 0.6 dynamic_slice.14
  55.6 3.7 %fusion.30 = f32[16,512,128]{2,1,0:T(8,128)} fusion(f32[16,512,128]{2,1,0:T(8,128)} %get-tuple-element.184, s32[]{:T(128)} %get-tuple-element.183, bf16[4096,128]{1,0:T(8,128)(2,1)S(1)} %get-tuple-element.194, s32[512]{0:T(512)S(1)} %iota_add_fusion.2, s32[4096]{0:T(1024)S(1)} %bitcast.45), kind=kOutput, calls=%fused_computation.14.clone.1 | convolution fusion | flops 538968064 | bytes 1329664 | tf_op jit(solution)/shard_map/while/body/eval_jaxpr/sr,sw->rw/dot_general | solution.py:23
  59.2 0.6 dynamic_slice.14
  60.5 3.7 %fusion.30 = f32[16,512,128]{2,1,0:T(8,128)} fusion(f32[16,512,128]{2,1,0:T(8,128)} %get-tuple-element.184, s32[]{:T(128)} %get-tuple-element.183, bf16[4096,128]{1,0:T(8,128)(2,1)S(1)} %get-tuple-element.194, s32[512]{0:T(512)S(1)} %iota_add_fusion.2, s32[4096]{0:T(1024)S(1)} %bitcast.45), kind=kOutput, calls=%fused_computation.14.clone.1 | convolution fusion | flops 538968064 | bytes 1329664 | tf_op jit(solution)/shard_map/while/body/eval_jaxpr/sr,sw->rw/dot_general | solution.py:23
  64.1 0.6 dynamic_slice.14
  65.4 3.7 %fusion.30 = f32[16,512,128]{2,1,0:T(8,128)} fusion(f32[16,512,128]{2,1,0:T(8,128)} %get-tuple-element.184, s32[]{:T(128)} %get-tuple-element.183, bf16[4096,128]{1,0:T(8,128)(2,1)S(1)} %get-tuple-element.194, s32[512]{0:T(512)S(1)} %iota_add_fusion.2, s32[4096]{0:T(1024)S(1)} %bitcast.45), kind=kOutput, calls=%fused_computation.14.clone.1 | convolution fusion | flops 538968064 | bytes 1329664 | tf_op jit(solution)/shard_map/while/body/eval_jaxpr/sr,sw->rw/dot_general | solution.py:23
  69.0 0.6 dynamic_slice.14
  70.3 3.7 %fusion.30 = f32[16,512,128]{2,1,0:T(8,128)} fusion(f32[16,512,128]{2,1,0:T(8,128)} %get-tuple-element.184, s32[]{:T(128)} %get-tuple-element.183, bf16[4096,128]{1,0:T(8,128)(2,1)S(1)} %get-tuple-element.194, s32[512]{0:T(512)S(1)} %iota_add_fusion.2, s32[4096]{0:T(1024)S(1)} %bitcast.45), kind=kOutput, calls=%fused_computation.14.clone.1 | convolution fusion | flops 538968064 | bytes 1329664 | tf_op jit(solution)/shard_map/while/body/eval_jaxpr/sr,sw->rw/dot_general | solution.py:23
  73.9 0.6 dynamic_slice.14
  75.2 3.7 %fusion.30 = f32[16,512,128]{2,1,0:T(8,128)} fusion(f32[16,512,128]{2,1,0:T(8,128)} %get-tuple-element.184, s32[]{:T(128)} %get-tuple-element.183, bf16[4096,128]{1,0:T(8,128)(2,1)S(1)} %get-tuple-element.194, s32[512]{0:T(512)S(1)} %iota_add_fusion.2, s32[4096]{0:T(1024)S(1)} %bitcast.45), kind=kOutput, calls=%fused_computation.14.clone.1 | convolution fusion | flops 538968064 | bytes 1329664 | tf_op jit(solution)/shard_map/while/body/eval_jaxpr/sr,sw->rw/dot_general | solution.py:23
  78.8 0.6 dynamic_slice.14
  80.1 3.7 %fusion.30 = f32[16,512,128]{2,1,0:T(8,128)} fusion(f32[16,512,128]{2,1,0:T(8,128)} %get-tuple-element.184, s32[]{:T(128)} %get-tuple-element.183, bf16[4096,128]{1,0:T(8,128)(2,1)S(1)} %get-tuple-element.194, s32[512]{0:T(512)S(1)} %iota_add_fusion.2, s32[4096]{0:T(1024)S(1)} %bitcast.45), kind=kOutput, calls=%fused_computation.14.clone.1 | convolution fusion | flops 538968064 | bytes 1329664 | tf_op jit(solution)/shard_map/while/body/eval_jaxpr/sr,sw->rw/dot_general | solution.py:23
  83.8 0.6 dynamic_slice.14
  85.0 3.7 %fusion.30 = f32[16,512,128]{2,1,0:T(8,128)} fusion(f32[16,512,128]{2,1,0:T(8,128)} %get-tuple-element.184, s32[]{:T(128)} %get-tuple-element.183, bf16[4096,128]{1,0:T(8,128)(2,1)S(1)} %get-tuple-element.194, s32[512]{0:T(512)S(1)} %iota_add_fusion.2, s32[4096]{0:T(1024)S(1)} %bitcast.45), kind=kOutput, calls=%fused_computation.14.clone.1 | convolution fusion | flops 538968064 | bytes 1329664 | tf_op jit(solution)/shard_map/while/body/eval_jaxpr/sr,sw->rw/dot_general | solution.py:23
  88.7 0.6 dynamic_slice.14
  89.9 3.7 %fusion.30 = f32[16,512,128]{2,1,0:T(8,128)} fusion(f32[16,512,128]{2,1,0:T(8,128)} %get-tuple-element.184, s32[]{:T(128)} %get-tuple-element.183, bf16[4096,128]{1,0:T(8,128)(2,1)S(1)} %get-tuple-element.194, s32[512]{0:T(512)S(1)} %iota_add_fusion.2, s32[4096]{0:T(1024)S(1)} %bitcast.45), kind=kOutput, calls=%fused_computation.14.clone.1 | convolution fusion | flops 538968064 | bytes 1329664 | tf_op jit(solution)/shard_map/while/body/eval_jaxpr/sr,sw->rw/dot_general | solution.py:23
  93.6 0.6 dynamic_slice.14
  94.8 3.7 %fusion.30 = f32[16,512,128]{2,1,0:T(8,128)} fusion(f32[16,512,128]{2,1,0:T(8,128)} %get-tuple-element.184, s32[]{:T(128)} %get-tuple-element.183, bf16[4096,128]{1,0:T(8,128)(2,1)S(1)} %get-tuple-element.194, s32[512]{0:T(512)S(1)} %iota_add_fusion.2, s32[4096]{0:T(1024)S(1)} %bitcast.45), kind=kOutput, calls=%fused_computation.14.clone.1 | convolution fusion | flops 538968064 | bytes 1329664 | tf_op jit(solution)/shard_map/while/body/eval_jaxpr/sr,sw->rw/dot_general | solution.py:23
  98.5 0.6 dynamic_slice.14
  99.7 3.7 %fusion.30 = f32[16,512,128]{2,1,0:T(8,128)} fusion(f32[16,512,128]{2,1,0:T(8,128)} %get-tuple-element.184, s32[]{:T(128)} %get-tuple-element.183, bf16[4096,128]{1,0:T(8,128)(2,1)S(1)} %get-tuple-element.194, s32[512]{0:T(512)S(1)} %iota_add_fusion.2, s32[4096]{0:T(1024)S(1)} %bitcast.45), kind=kOutput, calls=%fused_computation.14.clone.1 | convolution fusion | flops 538968064 | bytes 1329664 | tf_op jit(solution)/shard_map/while/body/eval_jaxpr/sr,sw->rw/dot_general | solution.py:23
  103.4 0.6 dynamic_slice.14
  104.6 3.7 %fusion.30 = f32[16,512,128]{2,1,0:T(8,128)} fusion(f32[16,512,128]{2,1,0:T(8,128)} %get-tuple-element.184, s32[]{:T(128)} %get-tuple-element.183, bf16[4096,128]{1,0:T(8,128)(2,1)S(1)} %get-tuple-element.194, s32[512]{0:T(512)S(1)} %iota_add_fusion.2, s32[4096]{0:T(1024)S(1)} %bitcast.45), kind=kOutput, calls=%fused_computation.14.clone.1 | convolution fusion | flops 538968064 | bytes 1329664 | tf_op jit(solution)/shard_map/while/body/eval_jaxpr/sr,sw->rw/dot_general | solution.py:23
  108.3 0.6 dynamic_slice.14
  109.6 3.7 %fusion.30 = f32[16,512,128]{2,1,0:T(8,128)} fusion(f32[16,512,128]{2,1,0:T(8,128)} %get-tuple-element.184, s32[]{:T(128)} %get-tuple-element.183, bf16[4096,128]{1,0:T(8,128)(2,1)S(1)} %get-tuple-element.194, s32[512]{0:T(512)S(1)} %iota_add_fusion.2, s32[4096]{0:T(1024)S(1)} %bitcast.45), kind=kOutput, calls=%fused_computation.14.clone.1 | convolution fusion | flops 538968064 | bytes 1329664 | tf_op jit(solution)/shard_map/while/body/eval_jaxpr/sr,sw->rw/dot_general | solution.py:23
  113.2 0.6 dynamic_slice.14
  114.5 3.7 %fusion.30 = f32[16,512,128]{2,1,0:T(8,128)} fusion(f32[16,512,128]{2,1,0:T(8,128)} %get-tuple-element.184, s32[]{:T(128)} %get-tuple-element.183, bf16[4096,128]{1,0:T(8,128)(2,1)S(1)} %get-tuple-element.194, s32[512]{0:T(512)S(1)} %iota_add_fusion.2, s32[4096]{0:T(1024)S(1)} %bitcast.45), kind=kOutput, calls=%fused_computation.14.clone.1 | convolution fusion | flops 538968064 | bytes 1329664 | tf_op jit(solution)/shard_map/while/body/eval_jaxpr/sr,sw->rw/dot_general | solution.py:23
  118.1 0.6 dynamic_slice.14
  119.4 3.7 %fusion.30 = f32[16,512,128]{2,1,0:T(8,128)} fusion(f32[16,512,128]{2,1,0:T(8,128)} %get-tuple-element.184, s32[]{:T(128)} %get-tuple-element.183, bf16[4096,128]{1,0:T(8,128)(2,1)S(1)} %get-tuple-element.194, s32[512]{0:T(512)S(1)} %iota_add_fusion.2, s32[4096]{0:T(1024)S(1)} %bitcast.45), kind=kOutput, calls=%fused_computation.14.clone.1 | convolution fusion | flops 538968064 | bytes 1329664 | tf_op jit(solution)/shard_map/while/body/eval_jaxpr/sr,sw->rw/dot_general | solution.py:23
  123.0 0.0 copy-start.1
  123.0 0.0 all-reduce.2.cloned.1.call-update
  123.0 157.3 %all-reduce.2.cloned.1.call-done = f32[2,4096,128]{2,1,0:T(8,128)} async-done(((f32[2,4096,128]{2,1,0:T(8,128)}), f32[2,4096,128]{2,1,0:T(8,128)}) %all-reduce.2.cloned.1.call-update) | async-done | bytes 4194320 | tf_op jit(solution)/shard_map/psum | solution.py:70
  280.4 0.0 copy-start
  280.4 3.5 %multiply_reduce_fusion = f32[2,4096]{1,0:T(2,128)S(1)} fusion(f32[2,4096,128]{2,1,0:T(8,128)} %all-reduce.2.cloned.1.call-done), kind=kLoop, calls=%fused_computation.18 | loop fusion | flops 2088960 | bytes 4227072 | tf_op jit(solution)/shard_map/reduce_sum | solution.py:45
  283.9 0.0 copy-done.1
  283.9 0.7 sqrt_add_fusion
  284.6 0.0 copy-done
  284.6 4.2 %divide_subtract_fusion = f32[2,4096,128]{2,1,0:T(8,128)} fusion(f32[2,4096,128]{2,1,0:T(8,128)} %param.14, f32[2,4096,128]{2,1,0:T(8,128)S(1)} %copy-done, f32[2,4096]{1,0:T(2,128)S(1)} %get-tuple-element.103), kind=kLoop, calls=%fused_computation.17 | loop fusion | flops 3145728 | bytes 12615680 | tf_op jit(solution)/shard_map/sub | solution.py:46
  (40 shorter events, 0.2 us)
Async XLA Ops:
  8.6 18.0 %all-to-all-start = ((s32[4,1,1024]{2,1,0:T(1,128)}), s32[4,1,1024]{2,1,0:T(1,128)S(1)}, u32[]{:S(2)}, u32[]{:S(2)}) async-start(s32[4,1,1024]{2,1,0:T(1,128)} %compare_select_fusion), calls=%async_computation | async-start | bytes 32768 | tf_op jit(solution)/shard_map/all_to_all | solution.py:67
  26.6 17.9 %all-to-all-start.1 = ((bf16[4,1024,128]{2,1,0:T(8,128)(2,1)}), bf16[4,1024,128]{2,1,0:T(8,128)(2,1)S(1)}, u32[]{:S(2)}, u32[]{:S(2)}) async-start(bf16[4,1024,128]{2,1,0:T(8,128)(2,1)} %get-tuple-element.61), calls=%async_computation.1 | async-start | bytes 2097152 | tf_op jit(solution)/shard_map/all_to_all | solution.py:66
  30.1 250.3 %all-reduce.2.cloned.1.call-start = ((), (), s32[]{:S(2)}) async-start(), calls=%async_computation.2 | async-start | bytes 8388608 | tf_op jit(solution)/shard_map/psum | solution.py:70
  123.0 160.9 %copy-start.1 = (f32[2,4096]{1,0:T(2,128)S(1)}, f32[2,4096]{1,0:T(2,128)}, u32[]{:S(2)}) copy-start(f32[2,4096]{1,0:T(2,128)} %param.15) | copy-start | bytes 98308
  280.4 4.2 %copy-start = (f32[2,4096,128]{2,1,0:T(8,128)S(1)}, f32[2,4096,128]{2,1,0:T(8,128)}, u32[]{:S(2)}) copy-start(f32[2,4096,128]{2,1,0:T(8,128)} %all-reduce.2.cloned.1.call-done) | copy-start | bytes 12582916
Sparse Core Ops, SparseCore 0:
  123.2 157.1 all-reduce.1
where the time goes:
time: 296 us
  waiting for transfers between devices  172 us (58%)
  matrix products  71.3 us (24%)
  between operations  14.1 us (5%)
  loops' own time  10.7 us (4%)
  other arithmetic  10.6 us (4%)
  local copies, waits for them, and re-layouts  9.41 us (3%)
  starting transfers between devices  7.82 us (3%)
    psum x1, waiting for transfers between devices, shards(): row_grad = lax.psum(partial_grad, 'rep')  157 us
    dot_general x16, matrix products, row_block(): jnp.einsum('sr,sw->rw', matches, flat_rows, preferred_element_type=jnp.fl...  58.4 us
    all_to_all x1, waiting for transfers between devices, shards(): lax.all_to_all(picked, 'rows', split_axis=0, concat_axis=0, tiled=True)  14.3 us
    dot_general x4, matrix products, slot_block(): jnp.dot(matches, flat_grad, preferred_element_type=jnp.float32)  12.9 us
    another operation x1, loops' own time, accumulate(): blocks = lax.map(row_block, jnp.arange(block_count, dtype=jnp.int32))  10.7 us
    dynamic_slice x16, local copies, waits for them, and re-layouts, accumulate(): blocks = lax.map(row_block, jnp.arange(block_count, dtype=jnp.int32))  9.32 us
  transfers between devices with their start and end apart: 3, of which 2 were waited for; matrix products, arithmetic and copies ran while one was open for 5% of the time, Pallas kernels for 0%

commit v1 on v0

--- a/solution.py
+++ b/solution.py
@@ -67,7 +67,9 @@
         lax.all_to_all(targets, "rows", split_axis=0, concat_axis=0, tiled=True),
     )
     partial_grad = accumulate(got_grads, got_targets, tables, rows_dev)
-    row_grad = lax.psum(partial_grad, "rep")
+    row_grad = partial_grad
+    for hop in (1, 2, 4):
+        row_grad = row_grad + lax.ppermute(row_grad, "rep", [(dev, dev ^ hop) for dev in range(8)])
     new_rows, new_accum = adagrad(table_rows, accum, row_grad)
     return (new_rows, new_accum)
 

time: 296 us -> 491 us (1.66)
  waiting for transfers between devices: 172 us -> 373 us
  between operations: 14.1 us -> 0.69 us
  starting transfers between devices: 7.82 us -> 14.3 us
    ppermute x0 -> x3, waiting for transfers between devices: none -> 359 us  [shards(): lax.ppermute(row_grad, 'rep', [(dev, dev ^ hop) for dev in range(8)])]
    psum x1 -> x0, waiting for transfers between devices: 157 us -> none  [shards(): row_grad = lax.psum(partial_grad, 'rep')]
    ppermute x0 -> x3, starting transfers between devices: none -> 6.55 us  [shards(): lax.ppermute(row_grad, 'rep', [(dev, dev ^ hop) for dev in range(8)])]
  transfers between devices with their start and end apart: 3 -> 5, of which waited for: 2 -> 4; matrix products, arithmetic and copies ran while one was open for 5% -> 3% of each run, Pallas kernels for 0% -> 0%
where the time goes in v1:
time: 491 us; the launch traced here: 490 us
  waiting for transfers between devices  373 us (76%)
  matrix products  71.3 us (15%)
  starting transfers between devices  14.3 us (3%)
  loops' own time  10.7 us (2%)
  other arithmetic  10.4 us (2%)
  local copies, waits for them, and re-layouts  9.42 us (2%)
    ppermute x3, waiting for transfers between devices, shards(): lax.ppermute(row_grad, 'rep', [(dev, dev ^ hop) for dev in range(8)])  359 us
    dot_general x16, matrix products, row_block(): jnp.einsum('sr,sw->rw', matches, flat_rows, preferred_element_type=jnp.fl...  58.4 us
    all_to_all x1, waiting for transfers between devices, shards(): lax.all_to_all(picked, 'rows', split_axis=0, concat_axis=0, tiled=True)  14.4 us
    dot_general x4, matrix products, slot_block(): jnp.dot(matches, flat_grad, preferred_element_type=jnp.float32)  12.9 us
    another operation x1, loops' own time, accumulate(): blocks = lax.map(row_block, jnp.arange(block_count, dtype=jnp.int32))  10.7 us
  transfers between devices with their start and end apart: 5, of which 4 were waited for; matrix products, arithmetic and copies ran while one was open for 3% of the time, Pallas kernels for 0%

profile of v1, /device:TPU:0, one launch (start us, length us, event | category | flops | bytes accessed | tf_op | source)
XLA Modules:
  0.0 490.0 jit_solution(15269057772257923536)
XLA Ops:
  0.6 1.4 compare_select_fusion
  2.0 4.3 all-to-all-start
  6.3 0.8 bitcast_select_fusion
  7.1 12.9 %while.22 = (s32[]{:T(128)}, bf16[4,1024,128]{2,1,0:T(8,128)(2,1)}, s32[4,1024]{1,0:T(4,128)S(1)}, bf16[2048,128]{1,0:T(8,128)(2,1)}, s32[]{:T(128)}) while((s32[]{:T(128)}, bf16[4,1024,128]{2,1,0:T(8,128)(2,1)}, s32[4,1024]{1,0:T(4,128)S(1)}, bf16[2048,128]{1,0:T(8,128)(2,1)}, s32[]{:T(128)}) %tuple.50), condition=%wide.region_1.2_spmd.clone, body=%wide.region_0.1_spmd.clone.sunk | while | flops 539099136 | bytes 798797 | solution.py:40
  7.1 3.2 fusion.27
  10.3 3.2 fusion.27
  13.6 3.2 fusion.27
  16.8 3.2 fusion.27
  20.0 0.0 all-to-all-done
  20.0 3.5 all-to-all-start.1
  23.6 14.4 %all-to-all-done.1 = bf16[4,1024,128]{2,1,0:T(8,128)(2,1)S(1)} async-done(((bf16[4,1024,128]{2,1,0:T(8,128)(2,1)}), bf16[4,1024,128]{2,1,0:T(8,128)(2,1)S(1)}, u32[]{:S(2)}, u32[]{:S(2)}) %all-to-all-start.1) | async-done | bytes 1048608 | tf_op jit(solution)/shard_map/all_to_all | solution.py:66
  37.9 78.5 %while.23 = (s32[]{:T(128)}, f32[16,512,128]{2,1,0:T(8,128)}, s32[4,1024]{1,0:T(4,128)S(1)}, s32[16]{0:T(128)S(1)}, bf16[4096,128]{1,0:T(8,128)(2,1)S(1)}, /*index=5*/s32[]{:T(128)}, s32[1]{0:T(128)}) while((s32[]{:T(128)}, f32[16,512,128]{2,1,0:T(8,128)}, s32[4,1024]{1,0:T(4,128)S(1)}, s32[16]{0:T(128)S(1)}, ...), condition=%wide.region_3.4_spmd.clone, body=%wide.region_2.3_spmd.clone.sunk | while | flops 538968576 | bytes 1364085 | solution.py:25
  37.9 0.6 dynamic_slice.14
  39.2 3.7 fusion.30
  42.9 0.6 dynamic_slice.14
  44.1 3.7 fusion.30
  47.8 0.6 dynamic_slice.14
  49.0 3.7 fusion.30
  52.7 0.6 dynamic_slice.14
  53.9 3.7 fusion.30
  57.6 0.6 dynamic_slice.14
  58.8 3.7 fusion.30
  62.5 0.6 dynamic_slice.14
  63.8 3.7 fusion.30
  67.4 0.6 dynamic_slice.14
  68.7 3.7 fusion.30
  72.3 0.6 dynamic_slice.14
  73.6 3.7 fusion.30
  77.2 0.6 dynamic_slice.14
  78.5 3.7 fusion.30
  82.1 0.6 dynamic_slice.14
  83.4 3.7 fusion.30
  87.0 0.6 dynamic_slice.14
  88.3 3.7 fusion.30
  91.9 0.6 dynamic_slice.14
  93.2 3.7 fusion.30
  96.9 0.6 dynamic_slice.14
  98.1 3.7 fusion.30
  101.8 0.6 dynamic_slice.14
  103.0 3.7 fusion.30
  106.7 0.6 dynamic_slice.14
  107.9 3.7 fusion.30
  111.6 0.6 dynamic_slice.14
  112.8 3.7 fusion.30
  116.5 2.0 collective-permute-start
  118.5 90.5 %collective-permute-done = f32[2,4096,128]{2,1,0:T(8,128)S(1)} collective-permute-done((f32[2,4096,128]{2,1,0:T(8,128)}, f32[2,4096,128]{2,1,0:T(8,128)S(1)}, u32[]{:S(2)}, u32[]{:S(2)}) %collective-permute-start) | collective-permute-done | bytes 4194336 | tf_op jit(solution)/shard_map/ppermute | solution.py:72
  208.9 2.7 bitcast_add_fusion
  211.7 1.9 collective-permute-start.1
  213.5 89.6 %collective-permute-done.1 = f32[2,4096,128]{2,1,0:T(8,128)S(1)} collective-permute-done((f32[2,4096,128]{2,1,0:T(8,128)S(1)}, f32[2,4096,128]{2,1,0:T(8,128)S(1)}, u32[]{:S(2)}, u32[]{:S(2)}) %collective-permute-start.1) | collective-permute-done | bytes 4194336 | tf_op jit(solution)/shard_map/ppermute | solution.py:72
  303.1 0.4 add.37
  303.5 0.0 copy-start.1
  303.5 0.0 copy-start
  303.5 2.7 collective-permute-start.2
  306.2 178.7 %collective-permute-done.2 = f32[2,4096,128]{2,1,0:T(8,128)S(1)} collective-permute-done((f32[2,4096,128]{2,1,0:T(8,128)S(1)}, f32[2,4096,128]{2,1,0:T(8,128)S(1)}, u32[]{:S(2)}, u32[]{:S(2)}) %collective-permute-start.2) | collective-permute-done | bytes 4194336 | tf_op jit(solution)/shard_map/ppermute | solution.py:72
  484.9 1.2 multiply_reduce_fusion
  486.1 0.0 copy-done.1
  486.1 0.7 sqrt_add_fusion
  486.8 0.0 copy-done
  486.8 3.2 divide_subtract_fusion
  (40 shorter events, 0.2 us)
Async XLA Ops:
  2.0 18.0 %all-to-all-start = ((s32[4,1,1024]{2,1,0:T(1,128)}), s32[4,1,1024]{2,1,0:T(1,128)S(1)}, u32[]{:S(2)}, u32[]{:S(2)}) async-start(s32[4,1,1024]{2,1,0:T(1,128)} %compare_select_fusion), calls=%async_computation | async-start | bytes 32768 | tf_op jit(solution)/shard_map/all_to_all | solution.py:67
  20.0 17.9 %all-to-all-start.1 = ((bf16[4,1024,128]{2,1,0:T(8,128)(2,1)}), bf16[4,1024,128]{2,1,0:T(8,128)(2,1)S(1)}, u32[]{:S(2)}, u32[]{:S(2)}) async-start(bf16[4,1024,128]{2,1,0:T(8,128)(2,1)} %get-tuple-element.61), calls=%async_computation.1 | async-start | bytes 2097152 | tf_op jit(solution)/shard_map/all_to_all | solution.py:66
  116.5 92.5 %collective-permute-start = (f32[2,4096,128]{2,1,0:T(8,128)}, f32[2,4096,128]{2,1,0:T(8,128)S(1)}, u32[]{:S(2)}, u32[]{:S(2)}) collective-permute-start(f32[2,4096,128]{2,1,0:T(8,128)} %bitcast.43), channel_id=1, source_target_pairs={{0,4},{4,0},{8,12},{12,8},{16,20},{20,16},{24,28},{28,24},{1,5},{5... | collective-permute-start | bytes 12582920 | tf_op jit(solution)/shard_map/ppermute | solution.py:72
  211.7 91.5 %collective-permute-start.1 = (f32[2,4096,128]{2,1,0:T(8,128)S(1)}, f32[2,4096,128]{2,1,0:T(8,128)S(1)}, u32[]{:S(2)}, u32[]{:S(2)}) collective-permute-start(f32[2,4096,128]{2,1,0:T(8,128)S(1)} %bitcast_add_fusion), channel_id=1, source_target_pairs={{0,8},{4,12},{8,0},{12,4},{16,24},{20,28},{24,16},{28,20},{1,9},{5... | collective-permute-start | bytes 12582920 | tf_op jit(solution)/shard_map/ppermute | solution.py:72
  303.5 182.6 %copy-start.1 = (f32[2,4096]{1,0:T(2,128)S(1)}, f32[2,4096]{1,0:T(2,128)}, u32[]{:S(2)}) copy-start(f32[2,4096]{1,0:T(2,128)} %param.15) | copy-start | bytes 98308
  303.5 183.3 %copy-start = (f32[2,4096,128]{2,1,0:T(8,128)S(1)}, f32[2,4096,128]{2,1,0:T(8,128)}, u32[]{:S(2)}) copy-start(f32[2,4096,128]{2,1,0:T(8,128)} %param.14) | copy-start | bytes 12582916
  303.5 181.4 %collective-permute-start.2 = (f32[2,4096,128]{2,1,0:T(8,128)S(1)}, f32[2,4096,128]{2,1,0:T(8,128)S(1)}, u32[]{:S(2)}, u32[]{:S(2)}) collective-permute-start(f32[2,4096,128]{2,1,0:T(8,128)S(1)} %add.37), channel_id=1, source_target_pairs={{0,16},{4,20},{8,24},{12,28},{16,0},{20,4},{24,8},{28,12},{1,17},{... | collective-permute-start | bytes 12582920 | tf_op jit(solution)/shard_map/ppermute | solution.py:72
